TPU v7x, 128 devices: a whole 4x4x4 slice. The times are simulated.
128 devices in a mesh: row: 32 (over y_lo, z, x), col: 4 (over y_hi, core).
Axes of the slice: x: 4, y: 4 (y_hi: 2, y_lo: 2; y = y_hi * 2 + y_lo), z: 4, core: 2. Of those that a mesh axis runs over, the one named last changes fastest.
Arguments:
- flow: bfloat16 [8192, 8192], P('row', 'col'), may hold values from 0.0009994507 to 1
- pattern: int32 [32, 32], P('row', 'col'), may hold values 0 or 1
- keep: int32 [32, 32], P('row', 'col'), may hold values 0 or 1
Outputs:
- clustered: float32 [8192, 8192], P('row', 'col')
All inputs are finite; a program needn't handle non-finite values. No bound on the sum of `pattern` or of `keep` on one device may be relied on, other than what follows from the above.
Results may differ from a plain program's by a relative error of at most 0.00046.
Values may be sent and summed in bfloat16 or wider, within the bound.
A program may use at most 128 MiB of HBM per device.

v0:
```python
import jax
import jax.numpy as jnp
from jax import lax
from jax.sharding import PartitionSpec as P


def spread_tiles(grid, tile):
    trows, tcols = grid.shape
    wide = jnp.broadcast_to(grid[:, None, :, None], (trows, tile, tcols, tile))
    return wide.reshape(trows * tile, tcols * tile)


def body(flow, pattern, keep):
    rows_dev, cols_dev = flow.shape
    trows, tcols = pattern.shape
    tile = rows_dev // trows
    row_start = lax.axis_index("row") * rows_dev
    col_start = lax.axis_index("col") * cols_dev
    global_rows = row_start + lax.iota(jnp.int32, rows_dev)
    global_cols = col_start + lax.iota(jnp.int32, cols_dev)
    loops = (global_rows[:, None] == global_cols[None, :]).astype(jnp.float32)
    base = flow.astype(jnp.float32) * spread_tiles((pattern > 0).astype(jnp.float32), tile) + loops
    mass = lax.psum(jnp.sum(base, axis=0), "row")
    stochastic = (base / mass[None, :]).astype(jnp.bfloat16)
    left = lax.all_gather(stochastic, "col", axis=1, tiled=True)
    right = lax.all_gather(stochastic, "row", axis=0, tiled=True)
    expanded = jnp.dot(left, right, preferred_element_type=jnp.float32)
    tile_rows = lax.axis_index("row") * trows + lax.iota(jnp.int32, trows)
    tile_cols = lax.axis_index("col") * tcols + lax.iota(jnp.int32, tcols)
    kept = jnp.logical_or(keep > 0, tile_rows[:, None] == tile_cols[None, :]).astype(jnp.float32)
    expanded = expanded * spread_tiles(kept, tile)
    inflated = expanded * expanded
    partial_totals = jnp.sum(inflated, axis=0)
    order = rows_dev * lax.axis_size("row")
    totals = lax.psum(partial_totals, "row")
    scale = order / totals
    return inflated * scale[None, :]


def solution(mesh):
    return jax.shard_map(
        body,
        mesh=mesh,
        in_specs=(P("row", "col"), P("row", "col"), P("row", "col")),
        out_specs=P("row", "col"),
        check_vma=False,
    )
```

profile of v0, /device:TPU:0, one launch (start us, length us, event | category | flops | bytes accessed | tf_op | source)
XLA Modules:
  0.0 601.0 jit_solution(7701374311171810818)
XLA Ops:
  6.5 0.0 all-gather.3.cloned.1.call-start
  6.5 0.7 fusion.2
  7.2 0.1 broadcast_bitcast_fusion.1
  7.3 1.7 fusion.1
  9.0 85.2 %psum.14 = f32[2048]{0:T(1024)S(1)} all-reduce(f32[2048]{0:T(1024)S(1)} %fusion.1), channel_id=1, replica_groups=mesh['row'=32,'col'=4] {'row'}, use_global_device_ids=true, to_apply=%region_1.0 | all-reduce | flops 2048 | bytes 16384 | tf_op jit(solution)/shard_map/psum | solution.py:23
  94.2 0.0 copy-start
  94.2 2.7 divide_convert_fusion
  96.9 0.0 all-gather.3.cloned.1.call-update
  96.9 0.0 all-gather.5.cloned.1.call-start
  97.0 0.7 all-gather.5.cloned.1.call-update
  97.7 0.0 copy-done
  97.7 0.1 broadcast_bitcast_fusion
  97.8 34.0 %all-gather.3.cloned.1.call-done = bf16[256,8192]{1,0:T(8,128)(2,1)} async-done(((bf16[256,2048]{1,0:T(8,128)(2,1)}), bf16[256,8192]{1,0:T(8,128)(2,1)}) %all-gather.3.cloned.1.call-update) | async-done | bytes 4194320 | tf_op jit(solution)/shard_map/all_gather | solution.py:25
  131.7 365.9 %all-gather.5.cloned.1.call-done = bf16[8192,2048]{1,0:T(8,128)(2,1)} async-done(((bf16[256,2048]{1,0:T(8,128)(2,1)}), bf16[8192,2048]{1,0:T(8,128)(2,1)}) %all-gather.5.cloned.1.call-update) | async-done | bytes 33554448 | tf_op jit(solution)/shard_map/all_gather | solution.py:26
  497.6 16.3 %fusion.4 = (f32[2048]{0:T(1024)S(1)}, f32[256,2048]{1,0:T(8,128)S(1)}) fusion(f32[2048]{0:T(1024)S(1)} %bitcast.14, bf16[256,8192]{1,0:T(8,128)(2,1)} %all-gather.3.cloned.1.call-done, bf16[8192,2048]{1,0:T(8,128)(2,1)} %all-gather.5.cloned.1.call-done), kind=kOutput, calls=%fused_computation.15 | convolution fusion | flops 8591505408 | bytes 39862272 | tf_op jit(solution)/shard_map/dot_general | solution.py:27
  513.9 78.7 %psum.15 = f32[2048]{0:T(1024)S(1)} all-reduce(f32[2048]{0:T(1024)S(1)} %get-tuple-element.5), channel_id=1, replica_groups=mesh['row'=32,'col'=4] {'row'}, use_global_device_ids=true, to_apply=%region_3.0 | all-reduce | flops 2048 | bytes 16384 | tf_op jit(solution)/shard_map/psum | solution.py:35
  592.6 1.6 broadcast_multiply_fusion
  (6 shorter events, 0.0 us)
Async XLA Ops:
  6.5 125.2 %all-gather.3.cloned.1.call-start = ((), (), s32[]{:S(2)}) async-start(), calls=%async_computation | async-start | bytes 5242880 | tf_op jit(solution)/shard_map/all_gather | solution.py:25
  94.2 3.5 copy-start
  96.9 400.7 %all-gather.5.cloned.1.call-start = ((), (), s32[]{:S(2)}) async-start(), calls=%async_computation.1 | async-start | bytes 34603008 | tf_op jit(solution)/shard_map/all_gather | solution.py:26
Sparse Core Ops, SparseCore 0:
  97.0 34.6 all-gather.2
  133.4 364.2 all-gather.4
where the time goes:
time: 601 us
  waiting for transfers between devices  401 us (67%)
  blocking collectives  164 us (27%)
  matrix products  16.3 us (3%)
  between operations  13.5 us (2%)
  other arithmetic  6.62 us (1%)
    all_gather x1, waiting for transfers between devices, body(): right = lax.all_gather(stochastic, 'row', axis=0, tiled=True)  366 us
    psum x1, blocking collectives, body(): mass = lax.psum(jnp.sum(base, axis=0), 'row')  85.2 us
    psum x1, blocking collectives, body(): totals = lax.psum(partial_totals, 'row')  78.7 us
    all_gather x1, waiting for transfers between devices, body(): left = lax.all_gather(stochastic, 'col', axis=1, tiled=True)  34 us
    dot_general x1, matrix products, body(): expanded = jnp.dot(left, right, preferred_element_type=jnp.float32)  16.3 us
  transfers between devices with their start and end apart: 2, of which 2 were waited for; matrix products, arithmetic and copies ran while one was open for 0% of the time, Pallas kernels for 0%

commit v1 on v0

--- a/solution.py
+++ b/solution.py
@@ -20,7 +20,9 @@
     global_cols = col_start + lax.iota(jnp.int32, cols_dev)
     loops = (global_rows[:, None] == global_cols[None, :]).astype(jnp.float32)
     base = flow.astype(jnp.float32) * spread_tiles((pattern > 0).astype(jnp.float32), tile) + loops
-    mass = lax.psum(jnp.sum(base, axis=0), "row")
+    block = jnp.sum(base, axis=0)
+    parts = lax.all_gather(block, "row")
+    mass = jnp.sum(parts, axis=0)
     stochastic = (base / mass[None, :]).astype(jnp.bfloat16)
     left = lax.all_gather(stochastic, "col", axis=1, tiled=True)
     right = lax.all_gather(stochastic, "row", axis=0, tiled=True)

time: 601 us -> 599 us (level)
    psum x1 -> x0, blocking collectives: 85.2 us -> none  [body(): mass = lax.psum(jnp.sum(base, axis=0), 'row')]
    all_gather x0 -> x1, blocking collectives: none -> 84 us  [body(): parts = lax.all_gather(block, 'row')]
where the time goes in v1:
time: 599 us
  waiting for transfers between devices  401 us (67%)
  blocking collectives  163 us (27%)
  matrix products  16.3 us (3%)
  between operations  13.5 us (2%)
    all_gather x1, waiting for transfers between devices, body(): right = lax.all_gather(stochastic, 'row', axis=0, tiled=True)  366 us
    all_gather x1, blocking collectives, body(): parts = lax.all_gather(block, 'row')  84 us
    psum x1, blocking collectives, body(): totals = lax.psum(partial_totals, 'row')  78.7 us
    all_gather x1, waiting for transfers between devices, body(): left = lax.all_gather(stochastic, 'col', axis=1, tiled=True)  34 us
    dot_general x1, matrix products, body(): expanded = jnp.dot(left, right, preferred_element_type=jnp.float32)  16.3 us
  transfers between devices with their start and end apart: 2, of which 2 were waited for; matrix products, arithmetic and copies ran while one was open for 0% of the time, Pallas kernels for 0%

profile of v1, /device:TPU:0, one launch (start us, length us, event | category | flops | bytes accessed | tf_op | source)
XLA Modules:
  0.0 598.7 jit_solution(3512231451956925856)
XLA Ops:
  6.5 0.0 copy-start
  6.5 0.0 all-gather.4.cloned.1.call-start
  6.5 0.7 fusion.2
  7.3 0.1 broadcast_bitcast_fusion.1
  7.4 1.7 fusion.1
  9.1 84.0 %all-gather = f32[65536]{0:T(1024)S(1)} all-gather(f32[2048]{0:T(1024)S(1)} %fusion.1), channel_id=2, replica_groups=mesh['row'=32,'col'=4] {'row'}, dimensions={0}, use_global_device_ids=true | all-gather | bytes 270336 | tf_op jit(solution)/shard_map/all_gather | solution.py:24
  93.1 0.0 copy-done
  93.1 0.0 copy-start.1
  93.1 1.5 divide_convert_fusion
  94.6 0.0 all-gather.4.cloned.1.call-update
  94.6 0.0 all-gather.6.cloned.1.call-start
  94.7 0.7 all-gather.6.cloned.1.call-update
  95.4 0.0 copy-done.1
  95.4 0.1 broadcast_bitcast_fusion
  95.5 34.0 %all-gather.4.cloned.1.call-done = bf16[256,8192]{1,0:T(8,128)(2,1)} async-done(((bf16[256,2048]{1,0:T(8,128)(2,1)}), bf16[256,8192]{1,0:T(8,128)(2,1)}) %all-gather.4.cloned.1.call-update) | async-done | bytes 4194320 | tf_op jit(solution)/shard_map/all_gather | solution.py:27
  129.5 365.9 %all-gather.6.cloned.1.call-done = bf16[8192,2048]{1,0:T(8,128)(2,1)} async-done(((bf16[256,2048]{1,0:T(8,128)(2,1)}), bf16[8192,2048]{1,0:T(8,128)(2,1)}) %all-gather.6.cloned.1.call-update) | async-done | bytes 33554448 | tf_op jit(solution)/shard_map/all_gather | solution.py:28
  495.4 16.3 %fusion.4 = (f32[2048]{0:T(1024)S(1)}, f32[256,2048]{1,0:T(8,128)S(1)}) fusion(f32[2048]{0:T(1024)S(1)} %bitcast.14, bf16[256,8192]{1,0:T(8,128)(2,1)} %all-gather.4.cloned.1.call-done, bf16[8192,2048]{1,0:T(8,128)(2,1)} %all-gather.6.cloned.1.call-done), kind=kOutput, calls=%fused_computation.15 | convolution fusion | flops 8591505408 | bytes 39862272 | tf_op jit(solution)/shard_map/dot_general | solution.py:29
  511.6 78.7 %psum.7 = f32[2048]{0:T(1024)S(1)} all-reduce(f32[2048]{0:T(1024)S(1)} %get-tuple-element.5), channel_id=1, replica_groups=mesh['row'=32,'col'=4] {'row'}, use_global_device_ids=true, to_apply=%region_3.0 | all-reduce | flops 2048 | bytes 16384 | tf_op jit(solution)/shard_map/psum | solution.py:37
  590.3 1.6 broadcast_multiply_fusion
  (8 shorter events, 0.1 us)
Async XLA Ops:
  6.5 86.6 %copy-start = (bf16[256,2048]{1,0:T(8,128)(2,1)S(1)}, bf16[256,2048]{1,0:T(8,128)(2,1)}, u32[]{:S(2)}) copy-start(bf16[256,2048]{1,0:T(8,128)(2,1)} %param.3) | copy-start | bytes 3145732
  6.5 122.9 %all-gather.4.cloned.1.call-start = ((), (), s32[]{:S(2)}) async-start(), calls=%async_computation | async-start | bytes 5242880 | tf_op jit(solution)/shard_map/all_gather | solution.py:27
  93.1 2.3 copy-start.1
  94.6 400.7 %all-gather.6.cloned.1.call-start = ((), (), s32[]{:S(2)}) async-start(), calls=%async_computation.1 | async-start | bytes 34603008 | tf_op jit(solution)/shard_map/all_gather | solution.py:28
Sparse Core Ops, SparseCore 0:
  94.7 34.6 all-gather.3
  131.1 364.2 all-gather.5
